TPU v7x, 32 devices: a whole 2x2x4 slice. The times are simulated.
32 devices in a mesh: dp: 16 (over z, y, x), tensor: 2 (over core).
Axes of the slice: x: 2, y: 2, z: 4, core: 2. Of those that a mesh axis runs over, the one named last changes fastest.
Arguments:
- images: bfloat16 [64, 256, 768], P(('dp', 'tensor')), may hold values from -6 to 6
- valid_count: int32 [64], P('dp'), may hold values from 16 to 256, as said below
- ln_gain: float32 [2, 2, 768], replicated, may hold values from 0.25 to 1.75
- ln_bias: float32 [2, 2, 768], replicated, may hold values from -1.5 to 1.5
- w_qkv: bfloat16 [2, 768, 3, 768], P(None, None, None, 'tensor'), may hold values from -0.21875 to 0.21875
- qv_bias: float32 [2, 2, 768], P(None, None, 'tensor'), may hold values from -2.5 to 2.5
- w_out: bfloat16 [2, 768, 768], P(None, 'tensor'), may hold values from -0.875 to 0.875
- out_bias: float32 [2, 2, 768], replicated, may hold values from -1.5 to 1.5
- w_up: bfloat16 [2, 768, 3072], P(None, None, 'tensor'), may hold values from -0.21875 to 0.21875
- up_bias: float32 [2, 3072], P(None, 'tensor'), may hold values from -1.5 to 1.5
- w_down: bfloat16 [2, 3072, 768], P(None, 'tensor'), may hold values from -0.109375 to 0.109375
- cotangent: bfloat16 [64, 256, 768], P(('dp', 'tensor')), may hold values from -6 to 6
Outputs:
- layer_out: float32 [64, 256, 768], P(('dp', 'tensor'))
- pooled: float32 [64, 768], P(('dp', 'tensor'))
- input_grad: float32 [64, 256, 768], P(('dp', 'tensor'))
- ln_gain_grad: float32 [2, 2, 768], replicated
- ln_bias_grad: float32 [2, 2, 768], replicated
- qkv_grad: float32 [2, 768, 3, 768], P(None, 'dp', None, 'tensor')
- qv_bias_grad: float32 [2, 2, 768], P(None, None, 'tensor')
- out_grad: float32 [2, 768, 768], P(None, 'tensor', 'dp')
- out_bias_grad: float32 [2, 2, 768], replicated
- up_grad: float32 [2, 768, 3072], P(None, 'dp', 'tensor')
- up_bias_grad: float32 [2, 3072], P(None, 'tensor')
- down_grad: float32 [2, 3072, 768], P(None, 'tensor', 'dp')
Inputs may be any that keep to these rules, and one draw needn't show every extreme that they name: `valid_count`: some image has exactly 256 valid patches and some other exactly 16; an image's valid patches are its first slots.
All inputs are finite; a program needn't handle non-finite values.
Results may differ from a plain program's by a relative error of at most 0.024.
Values may be sent and summed in bfloat16 or wider, within the bound.
No kernel may reach another device: no remote copies, remote signals or barrier semaphores. Data moves between devices by JAX's collectives and lax.ppermute only.
A program may use at most 192 MiB of HBM per device.

v0:
```python
import jax
import jax.numpy as jnp
from jax import lax
from jax.sharding import PartitionSpec as P

HEAD_DIM = 64
LAYERS = 2
EPSILON = 1e-06
NEGATIVE = -1e30


def normalize(values, norm_gain, norm_bias):
    average = jnp.mean(values, axis=-1, keepdims=True)
    centred = values - average
    variance = jnp.mean(centred * centred, axis=-1, keepdims=True)
    return centred * lax.rsqrt(variance + EPSILON) * norm_gain + norm_bias


def gelu_exact(values):
    return jax.nn.gelu(values, approximate=False)


def spread_rows(values):
    return lax.all_gather(values, "tensor", axis=0, tiled=True)


def spread_grads(values):
    return lax.all_gather(values, "tensor", axis=0, tiled=True)


def reduce_branch(left, weight, local_rows):

    def partial_term(start, count):
        return jnp.einsum("isn,nd->isd", left, weight, preferred_element_type=jnp.float32)

    return lax.psum_scatter(
        partial_term(jnp.int32(0), local_rows * lax.axis_size("tensor")).astype(jnp.bfloat16),
        "tensor",
        scatter_dimension=0,
        tiled=True,
    ).astype(jnp.float32)


def reduce_grads(left, weight, local_rows):

    def partial_term(start, count):
        return jnp.einsum("isn,dn->isd", left, weight, preferred_element_type=jnp.float32)

    return lax.psum_scatter(
        partial_term(jnp.int32(0), local_rows * lax.axis_size("tensor")).astype(jnp.bfloat16),
        "tensor",
        scatter_dimension=0,
        tiled=True,
    ).astype(jnp.float32)


def masked_scores(queries, keys_in, key_mask, score_scale):
    scores = (
        jnp.einsum("iqhe,ikhe->ihqk", queries, keys_in, preferred_element_type=jnp.float32)
        * score_scale
    )
    return jnp.where(key_mask[:, None, None, :], scores, NEGATIVE)


def attention_forward(queries, keys_in, values_in, key_mask, score_scale):
    scores = masked_scores(queries, keys_in, key_mask, score_scale)
    largest = jnp.max(scores, axis=-1, keepdims=True)
    exponent = jnp.exp(scores - largest)
    row_total = jnp.sum(exponent, axis=-1, keepdims=True)
    weights = (exponent / row_total).astype(jnp.bfloat16)
    attended = jnp.einsum("ihqk,ikhe->iqhe", weights, values_in, preferred_element_type=jnp.float32)
    return (attended.astype(jnp.bfloat16), largest + jnp.log(row_total))


def attention_backward(queries, keys_in, values_in, key_mask, log_total, grad_out, score_scale):
    scores = masked_scores(queries, keys_in, key_mask, score_scale)
    probs = jnp.exp(scores - log_total)
    grad_probs = jnp.einsum(
        "iqhe,ikhe->ihqk", grad_out, values_in, preferred_element_type=jnp.float32
    )
    grad_values = jnp.einsum(
        "ihqk,iqhe->ikhe", probs.astype(jnp.bfloat16), grad_out, preferred_element_type=jnp.float32
    )
    inner = jnp.sum(grad_probs * probs, axis=-1, keepdims=True)
    grad_scores = (probs * (grad_probs - inner)).astype(jnp.bfloat16)
    grad_queries = (
        jnp.einsum("ihqk,ikhe->iqhe", grad_scores, keys_in, preferred_element_type=jnp.float32)
        * score_scale
    )
    grad_keys = (
        jnp.einsum("ihqk,iqhe->ikhe", grad_scores, queries, preferred_element_type=jnp.float32)
        * score_scale
    )
    return (grad_queries, grad_keys, grad_values)


def shards(
    images,
    valid_count,
    ln_gain,
    ln_bias,
    w_qkv,
    qv_bias,
    w_out,
    out_bias,
    w_up,
    up_bias,
    w_down,
    cotangent,
):
    local_rows = images.shape[0]
    group_rows = valid_count.shape[0]
    slot_count = images.shape[1]
    width = images.shape[2]
    local_width = w_qkv.shape[3]
    head_count = local_width // HEAD_DIM
    score_scale = HEAD_DIM ** (-0.5)
    slot_index = jnp.arange(slot_count, dtype=jnp.int32)
    key_mask = slot_index[None, :] < valid_count[:, None]

    def split_heads(values):
        return values.reshape(group_rows, slot_count, head_count, HEAD_DIM)

    stream = images.astype(jnp.float32)
    saved = []
    for layer_index in range(LAYERS):
        first_in = stream
        first_rows = spread_rows(
            normalize(stream, ln_gain[layer_index, 0], ln_bias[layer_index, 0]).astype(jnp.bfloat16)
        )
        joint = jnp.einsum(
            "isd,dcn->iscn", first_rows, w_qkv[layer_index], preferred_element_type=jnp.float32
        )
        queries = split_heads((joint[:, :, 0] + qv_bias[layer_index, 0]).astype(jnp.bfloat16))
        keys_in = split_heads(joint[:, :, 1].astype(jnp.bfloat16))
        values_in = split_heads((joint[:, :, 2] + qv_bias[layer_index, 1]).astype(jnp.bfloat16))
        attended, log_total = attention_forward(queries, keys_in, values_in, key_mask, score_scale)
        attended = attended.reshape(group_rows, slot_count, local_width)
        stream = stream + (
            reduce_branch(attended, w_out[layer_index], local_rows) + out_bias[layer_index, 0]
        )
        second_in = stream
        second_rows = spread_rows(
            normalize(stream, ln_gain[layer_index, 1], ln_bias[layer_index, 1]).astype(jnp.bfloat16)
        )
        hidden_pre = (
            jnp.einsum(
                "isd,df->isf", second_rows, w_up[layer_index], preferred_element_type=jnp.float32
            )
            + up_bias[layer_index]
        )
        hidden = gelu_exact(hidden_pre).astype(jnp.bfloat16)
        stream = stream + (
            reduce_branch(hidden, w_down[layer_index], local_rows) + out_bias[layer_index, 1]
        )
        saved.append(
            (
                first_in,
                first_rows,
                queries,
                keys_in,
                values_in,
                log_total,
                attended,
                second_in,
                second_rows,
                hidden_pre,
                hidden,
            )
        )
    own_start = lax.axis_index("tensor") * local_rows
    own_counts = lax.dynamic_slice_in_dim(valid_count, own_start, local_rows)
    own_mask = slot_index[None, :] < own_counts[:, None]
    pooled = (
        jnp.sum(jnp.where(own_mask[:, :, None], stream, 0.0), axis=1)
        / own_counts.astype(jnp.float32)[:, None]
    )
    grad_stream = cotangent.astype(jnp.float32)
    weight_parts = [None] * LAYERS
    gain_parts = [None] * LAYERS
    shift_parts = [None] * LAYERS
    outb_parts = [None] * LAYERS
    qv_parts = [None] * LAYERS
    upb_parts = [None] * LAYERS
    for layer_index in reversed(range(LAYERS)):
        (
            first_in,
            first_rows,
            queries,
            keys_in,
            values_in,
            log_total,
            attended,
            second_in,
            second_rows,
            hidden_pre,
            hidden,
        ) = saved[layer_index]
        down_bias_grad = jnp.sum(grad_stream, axis=(0, 1))
        grad_rows = spread_grads(grad_stream.astype(jnp.bfloat16))
        down_grad = jnp.einsum("isf,isd->fd", hidden, grad_rows, preferred_element_type=jnp.float32)
        grad_hidden = jnp.einsum(
            "isd,fd->isf", grad_rows, w_down[layer_index], preferred_element_type=jnp.float32
        )
        grad_pre = jax.vjp(gelu_exact, hidden_pre)[1](grad_hidden)[0]
        hidden_bias_grad = jnp.sum(grad_pre, axis=(0, 1))
        grad_pre_low = grad_pre.astype(jnp.bfloat16)
        up_grad = jnp.einsum(
            "isd,isf->df", second_rows, grad_pre_low, preferred_element_type=jnp.float32
        )
        grad_normed = reduce_grads(grad_pre_low, w_up[layer_index], local_rows)
        grad_in, gain_second, shift_second = jax.vjp(
            normalize, second_in, ln_gain[layer_index, 1], ln_bias[layer_index, 1]
        )[1](grad_normed)
        grad_stream = grad_stream + grad_in
        proj_bias_grad = jnp.sum(grad_stream, axis=(0, 1))
        grad_rows = spread_grads(grad_stream.astype(jnp.bfloat16))
        out_grad = jnp.einsum(
            "isn,isd->nd", attended, grad_rows, preferred_element_type=jnp.float32
        )
        grad_att = jnp.einsum(
            "isd,nd->isn", grad_rows, w_out[layer_index], preferred_element_type=jnp.float32
        )
        grad_att = split_heads(grad_att.astype(jnp.bfloat16))
        grad_queries, grad_keys, grad_values = attention_backward(
            queries, keys_in, values_in, key_mask, log_total, grad_att, score_scale
        )
        grad_queries = grad_queries.reshape(group_rows, slot_count, local_width)
        grad_keys = grad_keys.reshape(group_rows, slot_count, local_width)
        grad_values = grad_values.reshape(group_rows, slot_count, local_width)
        qv_parts[layer_index] = jnp.stack(
            [jnp.sum(grad_queries, axis=(0, 1)), jnp.sum(grad_values, axis=(0, 1))]
        )
        grad_joint = jnp.stack([grad_queries, grad_keys, grad_values], axis=2).astype(jnp.bfloat16)
        qkv_grad = jnp.einsum(
            "isd,iscn->dcn", first_rows, grad_joint, preferred_element_type=jnp.float32
        )
        grad_normed = reduce_grads(
            grad_joint.reshape(group_rows, slot_count, 3 * local_width),
            w_qkv[layer_index].reshape(width, 3 * local_width),
            local_rows,
        )
        grad_in, gain_first, shift_first = jax.vjp(
            normalize, first_in, ln_gain[layer_index, 0], ln_bias[layer_index, 0]
        )[1](grad_normed)
        grad_stream = grad_stream + grad_in
        gain_parts[layer_index] = jnp.stack([gain_first, gain_second])
        shift_parts[layer_index] = jnp.stack([shift_first, shift_second])
        outb_parts[layer_index] = jnp.stack([proj_bias_grad, down_bias_grad])
        upb_parts[layer_index] = hidden_bias_grad
        layer_grads = (qkv_grad, out_grad, up_grad, down_grad)
        weight_parts[layer_index] = layer_grads
    stacked = tuple(
        (
            jnp.stack([weight_parts[layer_index][member] for layer_index in range(LAYERS)])
            for member in range(4)
        )
    )
    summed = (
        lax.psum_scatter(stacked[0], "dp", scatter_dimension=1, tiled=True),
        lax.psum_scatter(stacked[1], "dp", scatter_dimension=2, tiled=True),
        lax.psum_scatter(stacked[2], "dp", scatter_dimension=1, tiled=True),
        lax.psum_scatter(stacked[3], "dp", scatter_dimension=2, tiled=True),
    )
    qv_grads, upb_grads = lax.psum((jnp.stack(qv_parts), jnp.stack(upb_parts)), "dp")
    gain_grads, shift_grads, outb_grads = lax.psum(
        (jnp.stack(gain_parts), jnp.stack(shift_parts), jnp.stack(outb_parts)), ("dp", "tensor")
    )
    return (
        stream,
        pooled,
        grad_stream,
        gain_grads,
        shift_grads,
        summed[0],
        qv_grads,
        summed[1],
        outb_grads,
        summed[2],
        upb_grads,
        summed[3],
    )


def solution(mesh):
    placed = (
        P(("dp", "tensor"), None, None),
        P("dp"),
        P(),
        P(),
        P(None, None, None, "tensor"),
        P(None, None, "tensor"),
        P(None, "tensor", None),
        P(),
        P(None, None, "tensor"),
        P(None, "tensor"),
        P(None, "tensor", None),
        P(("dp", "tensor"), None, None),
    )
    return jax.shard_map(
        shards,
        mesh=mesh,
        in_specs=placed,
        out_specs=(
            P(("dp", "tensor"), None, None),
            P(("dp", "tensor"), None),
            P(("dp", "tensor"), None, None),
            P(),
            P(),
            P(None, "dp", None, "tensor"),
            P(None, None, "tensor"),
            P(None, "tensor", "dp"),
            P(),
            P(None, "dp", "tensor"),
            P(None, "tensor"),
            P(None, "tensor", "dp"),
        ),
        check_vma=False,
    )
```

profile of v0, /device:TPU:0, one launch (start us, length us, event | category | flops | bytes accessed | tf_op | source)
XLA Modules:
  0.0 1126.0 jit_solution(4967242549161505414)
XLA Ops:
  13.7 12.3 %all-gather.9.cloned.1.call-done = bf16[4,256,768]{2,1,0:T(8,128)(2,1)} async-done(((bf16[2,256,768]{2,1,0:T(8,128)(2,1)}), bf16[4,256,768]{2,1,0:T(8,128)(2,1)}) %all-gather.9.cloned.1.call-update) | async-done | bytes 1572880 | tf_op jit(solution)/shard_map/all_gather | solution.py:24
  26.1 4.2 fusion.60
  34.4 3.6 copy.102
  46.6 10.3 reduce-scatter.11.cloned.1.call-done
  61.7 10.8 all-gather.11.cloned.1.call-done
  72.6 6.3 fusion.95
  78.9 15.5 %multiply_convert_fusion.3 = (bf16[4,256,1536]{2,1,0:T(8,128)(2,1)S(1)}, f32[4,256,1536]{2,1,0:T(8,128)}) fusion(f32[4,256,1536]{2,1,0:T(8,128)S(1)} %get-tuple-element.122, f32[1536]{0:T(1024)S(1)} %get-tuple-element.73, u8[256,1536]{1,0:T(8,128)(4,1)S(1)} %get-tuple-element.51, u8[256,1536]{1,0:T(8,128)(4,1)S(1)} %get-tuple-element.50), kind=kLoop, calls=%fused_computation.40 | loop fusion | flops 111673344 | bytes 16521216 | tf_op jit(solution)/shard_map/convert_element_type | solution.py:152
  96.0 5.3 fusion.65
  101.3 10.3 reduce-scatter.13.cloned.1.call-done
  115.4 10.6 all-gather.13.cloned.1.call-done
  126.0 4.2 fusion.58
  151.5 10.3 reduce-scatter.15.cloned.1.call-done
  166.6 10.2 all-gather.15.cloned.1.call-done
  176.8 6.3 fusion.96
  185.8 15.6 %multiply_convert_fusion.2 = (bf16[4,256,1536]{2,1,0:T(8,128)(2,1)}, f32[4,256,1536]{2,1,0:T(8,128)}) fusion(f32[4,256,1536]{2,1,0:T(8,128)S(1)} %get-tuple-element.125, f32[1536]{0:T(1024)S(1)} %get-tuple-element.72, u8[256,1536]{1,0:T(8,128)(4,1)S(1)} %get-tuple-element.49, u8[256,1536]{1,0:T(8,128)(4,1)S(1)} %get-tuple-element.48), kind=kLoop, calls=%fused_computation.24 | loop fusion | flops 111673344 | bytes 16521216 | tf_op jit(solution)/shard_map/convert_element_type | solution.py:152
  201.4 10.2 fusion.134
  213.3 5.4 fusion.68
  218.7 6.4 fusion.71
  225.5 3.5 reduce-scatter.19.cloned.1.call-done
  232.3 9.1 reduce-scatter.17.cloned.1.call-done
  241.5 3.4 fusion.123
  247.1 4.2 fusion.131
  251.3 3.8 copy.120
  258.2 3.4 convolution_convert_fusion.5
  263.9 8.0 multiply_reduce_fusion.1
  271.9 4.5 multiply_convert_fusion.1
  293.3 4.3 copy.119
  297.6 5.6 convolution_convert_fusion.3
  303.7 9.9 reduce-scatter.21.cloned.1.call-done
  319.2 11.1 all-gather.21.cloned.1.call-done
  330.3 10.2 fusion.135
  342.3 5.4 fusion.62
  347.8 10.3 reduce-scatter.23.cloned.1.call-done
  366.5 8.7 all-gather.23.cloned.1.call-done
  375.2 3.6 convolution_convert_fusion.4
  381.1 5.4 multiply_reduce_fusion
  402.7 5.8 convolution_convert_fusion.2
  408.8 4.7 convolution_bitcast_fusion
  419.5 4.3 pad_maximum_fusion.1
  423.8 15.1 %copy.141 = f32[2,1536,768]{1,0,2:T(2,128)} copy(f32[2,1536,768]{2,1,0:T(8,128)} %pad_maximum_fusion.1) | data formatting | bytes 18874368 | tf_op jit(solution)/shard_map/stack | solution.py:255
  443.7 5.2 convolution_bitcast_fusion.2
  451.6 4.6 pad_maximum_fusion
  457.8 3.8 convolution_bitcast_fusion.4
  474.3 81.1 %all-reduce.3 = (f32[2,2,384]{2,1,0:T(2,128)}, f32[2,1536]{1,0:T(2,128)}) all-reduce(f32[2,2,384]{2,1,0:T(2,128)S(1)} %pad_maximum_fusion.10, f32[2,1536]{1,0:T(2,128)S(1)} %pad_maximum_fusion.9), channel_id=1, replica_groups=mesh['dp'=16,'tensor'=2] {'dp'}, use_global_device_ids=true, to_apply=%region_46.47 | all-reduce | flops 4608 | bytes 36864 | tf_op jit(solution)/shard_map/psum | solution.py:265
  559.4 39.5 %all-reduce.2 = (f32[2,2,768]{2,1,0:T(2,128)}, f32[2,2,768]{2,1,0:T(2,128)}, f32[2,2,768]{2,1,0:T(2,128)}) all-reduce(f32[2,2,768]{2,1,0:T(2,128)S(1)} %pad_maximum_fusion.6, f32[2,2,768]{2,1,0:T(2,128)S(1)} %pad_maximum_fusion.7, f32[2,2,768]{2,1,0:T(2,128)S(1)} %pad_maximum_fusion.8), channel_id=1, replica_groups=mesh['dp'=16,'tensor'=2] {'dp','tensor'}, use_global_device_ids=true, to_apply=%region_35.36 | all-reduce | flops 9216 | bytes 73728 | tf_op jit(solution)/shard_map/psum | solution.py:266
  600.6 186.0 %all-reduce.7.cloned.1.call-done = (f32[2,384,768]{1,0,2:T(2,128)}, f32[2,1536,768]{1,0,2:T(2,128)}) async-done(((f32[2,384,768]{1,0,2:T(2,128)}, f32[2,1536,768]{1,0,2:T(2,128)}), (f32[2,384,768]{1,0,2:T(2,128)}, f32[2,1536,768]{1,0,2:T(2,128)})) %all-reduce.7.cloned.1.call-update) | async-done | bytes 11796496
  790.3 173.4 %reduce-scatter.29.cloned.1.call-done = f32[2,48,1536]{2,1,0:T(8,128)} async-done(((f32[2,768,1536]{2,1,0:T(8,128)}), f32[2,48,1536]{2,1,0:T(8,128)}) %reduce-scatter.29.cloned.1.call-update) | async-done | bytes 589840 | tf_op jit(solution)/shard_map/reduce_scatter | solution.py:262
  963.7 155.3 %reduce-scatter.27.cloned.1.call-done = f32[2,48,3,384]{3,1,2,0:T(8,128)} async-done(((f32[2,768,3,384]{3,1,2,0:T(8,128)}), f32[2,48,3,384]{3,1,2,0:T(8,128)}) %reduce-scatter.27.cloned.1.call-update) | async-done | bytes 442384 | tf_op jit(solution)/shard_map/reduce_scatter | solution.py:260
  (331 shorter events, 158.9 us)
Async XLA Ops:
  7.2 6.3 copy-start.56
  7.2 6.5 copy-start.57
  7.2 18.9 %all-gather.9.cloned.1.call-start = ((), (), s32[]{:S(2)}) async-start(), calls=%async_computation.10 | async-start | bytes 2359296 | tf_op jit(solution)/shard_map/all_gather | solution.py:24
  8.6 21.7 %copy-start.46 = (f32[2,256]{1,0:T(2,128)}, f32[2,256]{1,0:T(2,128)S(1)}, u32[]{:S(2)}) copy-start(f32[2,256]{1,0:T(2,128)S(1)} %broadcast_multiply_fusion.3) | copy-start | bytes 6148
  10.1 20.2 %copy-start.52 = (f32[2,256]{1,0:T(2,128)}, f32[2,256]{1,0:T(2,128)S(1)}, u32[]{:S(2)}) copy-start(f32[2,256]{1,0:T(2,128)S(1)} %fusion.79) | copy-start | bytes 6148
  11.0 19.2 %copy-start.44 = (f32[768]{0:T(1024)}, f32[768]{0:T(1024)S(1)}, u32[]{:S(2)}) copy-start(f32[768]{0:T(1024)S(1)} %get-tuple-element.143) | copy-start | bytes 9220
  13.4 43.5 %reduce-scatter.11.cloned.1.call-start = ((), (), s32[]{:S(2)}) async-start(), calls=%async_computation.11 | async-start | bytes 2359296 | tf_op jit(solution)/shard_map/reduce_scatter | solution.py:36
  13.6 24.4 %copy-start.48 = (f32[6,64]{1,0:T(8,128)}, f32[6,64]{1,0:T(8,128)S(1)}, u32[]{:S(2)}) copy-start(f32[6,64]{1,0:T(8,128)S(1)} %add.272) | copy-start | bytes 4612
  34.4 5.0 copy-start.17
  44.3 12.6 %copy-start.2 = (bf16[2,256,768]{2,1,0:T(8,128)(2,1)S(1)}, bf16[2,256,768]{2,1,0:T(8,128)(2,1)}, u32[]{:S(2)}) copy-start(bf16[2,256,768]{2,1,0:T(8,128)(2,1)} %param.12) | copy-start | bytes 2359300
  46.5 26.1 %all-gather.11.cloned.1.call-start = ((), (), s32[]{:S(2)}) async-start(), calls=%async_computation.12 | async-start | bytes 2359296 | tf_op jit(solution)/shard_map/all_gather | solution.py:24
  61.4 50.2 %reduce-scatter.13.cloned.1.call-start = ((), (), s32[]{:S(2)}) async-start(), calls=%async_computation.13 | async-start | bytes 2359296 | tf_op jit(solution)/shard_map/reduce_scatter | solution.py:36
  78.9 15.5 %copy-start.26 = (f32[4,256,1536]{2,1,0:T(8,128)}, f32[4,256,1536]{2,1,0:T(8,128)S(1)}, u32[]{:S(2)}) copy-start(f32[4,256,1536]{2,1,0:T(8,128)S(1)} %get-tuple-element.122) | copy-start | bytes 18874372
  101.3 24.7 %all-gather.13.cloned.1.call-start = ((), (), s32[]{:S(2)}) async-start(), calls=%async_computation.14 | async-start | bytes 2359296 | tf_op jit(solution)/shard_map/all_gather | solution.py:24
  114.8 47.0 %reduce-scatter.15.cloned.1.call-start = ((), (), s32[]{:S(2)}) async-start(), calls=%async_computation.15 | async-start | bytes 2359296 | tf_op jit(solution)/shard_map/reduce_scatter | solution.py:36
  151.5 25.3 %all-gather.15.cloned.1.call-start = ((), (), s32[]{:S(2)}) async-start(), calls=%async_computation.16 | async-start | bytes 2359296 | tf_op jit(solution)/shard_map/all_gather | solution.py:24
  165.6 35.8 %all-gather.17.cloned.1.call-start = ((), (), s32[]{:S(2)}) async-start(), calls=%async_computation.18 | async-start | bytes 2359296 | tf_op jit(solution)/shard_map/all_gather | solution.py:28
  166.4 62.7 %reduce-scatter.19.cloned.1.call-start = ((), (), s32[]{:S(2)}) async-start(), calls=%async_computation.19 | async-start | bytes 2359296 | tf_op jit(solution)/shard_map/reduce_scatter | solution.py:49
  218.7 22.8 %reduce-scatter.17.cloned.1.call-start = ((), (), s32[]{:S(2)}) async-start(), calls=%async_computation.17 | async-start | bytes 2359296 | tf_op jit(solution)/shard_map/reduce_scatter | solution.py:36
  225.1 33.1 %all-gather.19.cloned.1.call-start = ((), (), s32[]{:S(2)}) async-start(), calls=%async_computation.20 | async-start | bytes 2359296 | tf_op jit(solution)/shard_map/all_gather | solution.py:28
  247.0 66.6 %reduce-scatter.21.cloned.1.call-start = ((), (), s32[]{:S(2)}) async-start(), calls=%async_computation.21 | async-start | bytes 2359296 | tf_op jit(solution)/shard_map/reduce_scatter | solution.py:49
  263.9 8.0 slice-start.2
  263.9 8.0 slice-start.3
  271.9 4.5 copy-start.18
  303.3 27.1 %all-gather.21.cloned.1.call-start = ((), (), s32[]{:S(2)}) async-start(), calls=%async_computation.22 | async-start | bytes 2359296 | tf_op jit(solution)/shard_map/all_gather | solution.py:28
  319.2 38.9 %reduce-scatter.23.cloned.1.call-start = ((), (), s32[]{:S(2)}) async-start(), calls=%async_computation.23 | async-start | bytes 2359296 | tf_op jit(solution)/shard_map/reduce_scatter | solution.py:49
  347.7 13.4 %copy-start.11 = (f32[2,256,768]{2,1,0:T(8,128)S(1)}, f32[2,256,768]{2,1,0:T(8,128)}, u32[]{:S(2)}) copy-start(f32[2,256,768]{2,1,0:T(8,128)} %copy-done.10) | copy-start | bytes 4718596
  347.7 27.5 %all-gather.23.cloned.1.call-start = ((), (), s32[]{:S(2)}) async-start(), calls=%async_computation.24 | async-start | bytes 2359296 | tf_op jit(solution)/shard_map/all_gather | solution.py:28
  364.0 191.3 %reduce-scatter.25.cloned.1.call-start = ((), (), s32[]{:S(2)}) async-start(), calls=%async_computation.25 | async-start | bytes 2359296 | tf_op jit(solution)/shard_map/reduce_scatter | solution.py:49
  375.2 11.3 slice-start
  381.1 5.4 slice-start.1
  381.1 5.4 copy-start.20
  402.7 6.1 copy-start.59
  408.5 5.0 copy-start.68
  408.5 378.1 %all-reduce.7.cloned.1.call-start = ((), (), s32[]{:S(2)}) async-start(), calls=%async_computation.28 | async-start | bytes 23592960
  408.8 4.8 copy-start.60
  423.8 15.1 %copy-start.62 = (bf16[4,256,768]{2,1,0:T(8,128)(2,1)S(1)}, bf16[4,256,768]{2,1,0:T(8,128)(2,1)}, u32[]{:S(2)}) copy-start(bf16[4,256,768]{2,1,0:T(8,128)(2,1)} %all-gather.23.cloned.1.call-done) | copy-start | bytes 4718596
  423.8 15.1 %copy-start.66 = (bf16[4,6,64,256]{3,2,1,0:T(8,128)(2,1)S(1)}, bf16[4,6,64,256]{3,2,1,0:T(8,128)(2,1)}, u32[]{:S(2)}) copy-start(bf16[4,6,64,256]{3,2,1,0:T(8,128)(2,1)} %copy-done.65) | copy-start | bytes 2359300
  443.4 5.5 copy-start.42
  443.4 520.3 %reduce-scatter.29.cloned.1.call-start = ((), (), s32[]{:S(2)}) async-start(), calls=%async_computation.27 | async-start | bytes 10027008 | tf_op jit(solution)/shard_map/reduce_scatter | solution.py:262
  443.7 5.2 copy-start.41
  456.2 662.8 %reduce-scatter.27.cloned.1.call-start = ((), (), s32[]{:S(2)}) async-start(), calls=%async_computation.26 | async-start | bytes 7520256 | tf_op jit(solution)/shard_map/reduce_scatter | solution.py:260
  470.1 85.2 %copy-start.45 = (f32[768]{0:T(1024)S(1)}, f32[768]{0:T(1024)}, u32[]{:S(2)}) copy-start(f32[768]{0:T(1024)} %copy-done.44) | copy-start | bytes 9220
  470.1 85.2 %copy-start.47 = (f32[2,256]{1,0:T(2,128)S(1)}, f32[2,256]{1,0:T(2,128)}, u32[]{:S(2)}) copy-start(f32[2,256]{1,0:T(2,128)} %copy-done.46) | copy-start | bytes 6148
  472.1 85.1 %copy-start.53 = (f32[2,256]{1,0:T(2,128)S(1)}, f32[2,256]{1,0:T(2,128)}, u32[]{:S(2)}) copy-start(f32[2,256]{1,0:T(2,128)} %copy-done.52) | copy-start | bytes 6148
  472.1 85.1 %copy-start.51 = (f32[2,256]{1,0:T(2,128)S(1)}, f32[2,256]{1,0:T(2,128)}, u32[]{:S(2)}) copy-start(f32[2,256]{1,0:T(2,128)} %copy-done.50) | copy-start | bytes 6148
  472.4 126.5 %copy-start.7 = (f32[2,256,768]{2,1,0:T(8,128)S(1)}, f32[2,256,768]{2,1,0:T(8,128)}, u32[]{:S(2)}) copy-start(f32[2,256,768]{2,1,0:T(8,128)} %copy-done.6) | copy-start | bytes 4718596
  555.4 43.6 %copy-start.24 = (bf16[2,256,768]{2,1,0:T(8,128)(2,1)S(1)}, bf16[2,256,768]{2,1,0:T(8,128)(2,1)}, u32[]{:S(2)}) copy-start(bf16[2,256,768]{2,1,0:T(8,128)(2,1)} %reduce-scatter.25.cloned.1.call-done) | copy-start | bytes 2359300
  (45 other events, 102.7 us)
Sparse Core Ops, SparseCore 0:
  13.5 12.4 all-gather.8
  46.6 10.2 reduce-scatter.10
  61.5 10.9 all-gather.10
  101.4 10.1 reduce-scatter.12
  114.9 11.0 all-gather.12
  151.6 10.2 reduce-scatter.14
  165.8 10.9 all-gather.14
  178.4 10.9 all-gather.16
  218.8 10.2 reduce-scatter.18
  231.2 10.2 reduce-scatter.16
  247.2 10.9 all-gather.18
  303.4 10.2 reduce-scatter.20
  319.3 10.9 all-gather.20
  347.8 10.2 reduce-scatter.22
  364.1 11.0 all-gather.22
  408.6 10.2 reduce-scatter.24
  443.5 343.0 all-reduce.6
  793.7 169.9 reduce-scatter.28
  969.6 149.3 reduce-scatter.26
where the time goes:
time: 1140 us; the launch traced here: 1130 us
  waiting for transfers between devices  646 us (57%)
  matrix products  144 us (13%)
  blocking collectives  121 us (11%)
  other arithmetic  99.7 us (9%)
  local copies, waits for them, and re-layouts  96.1 us (8%)
  between operations  16.3 us (1%)
    unnamed x20, waiting for transfers between devices  187 us
    reduce_scatter x1, waiting for transfers between devices, shards(): lax.psum_scatter(stacked[2], 'dp', scatter_dimension=1, tiled=True)  173 us
    reduce_scatter x1, waiting for transfers between devices, shards(): lax.psum_scatter(stacked[0], 'dp', scatter_dimension=1, tiled=True)  155 us
    psum x1, blocking collectives, shards(): lax.psum((jnp.stack(qv_parts), jnp.stack(upb_parts)), 'dp')  81.1 us
    all_gather x4, waiting for transfers between devices, spread_rows(): return lax.all_gather(values, 'tensor', axis=0, tiled=True)  43.9 us
    reduce_scatter x4, waiting for transfers between devices, reduce_branch(): lax.psum_scatter(partial_term(jnp.int32(0), local_rows * lax.axis_size('t...  40.1 us
    psum x1, blocking collectives, shards(): lax.psum((jnp.stack(gain_parts), jnp.stack(shift_parts), jnp.stack(outb_p...  39.5 us
    convert_element_type x2, other arithmetic, shards(): hidden = gelu_exact(hidden_pre).astype(jnp.bfloat16)  31.1 us
  transfers between devices with their start and end apart: 19, of which 17 were waited for; matrix products, arithmetic and copies ran while one was open for 10% of the time, Pallas kernels for 0%

commit v1 on v0

--- a/solution.py
+++ b/solution.py
@@ -21,7 +21,9 @@
 
 
 def spread_rows(values):
-    return lax.all_gather(values, "tensor", axis=0, tiled=True)
+    return jnp.concatenate(
+        lax.all_to_all(jnp.stack([values] * lax.axis_size("tensor")), "tensor", 0, 0), axis=0
+    )
 
 
 def spread_grads(values):

time: 1140 us -> 1110 us (0.974)
  waiting for transfers between devices: 646 us -> 602 us
  blocking collectives: 121 us -> 142 us
    all_gather x4 -> x0, waiting for transfers between devices: 43.9 us -> none  [spread_rows(): return lax.all_gather(values, 'tensor', axis=0, tiled=True)]
    all_to_all x0 -> x4, blocking collectives: none -> 21.5 us  [spread_rows(): lax.all_to_all(jnp.stack([values] * lax.axis_size('tensor')), 'tensor', 0...]
    unnamed x20 -> x16, waiting for transfers between devices: 187 us -> 186 us
    unnamed x153 -> x171, local copies, waits for them, and re-layouts: 25.3 us -> 25.6 us
  transfers between devices with their start and end apart: 19 -> 15, of which waited for: 17 -> 13; matrix products, arithmetic and copies ran while one was open for 10% -> 11% of each run, Pallas kernels for 0% -> 0%
where the time goes in v1:
time: 1110 us; the launch traced here: 1100 us
  waiting for transfers between devices  602 us (54%)
  blocking collectives  142 us (13%)
  matrix products  136 us (12%)
  other arithmetic  102 us (9%)
  local copies, waits for them, and re-layouts  102 us (9%)
  between operations  16.3 us (1%)
    unnamed x16, waiting for transfers between devices  186 us
    reduce_scatter x1, waiting for transfers between devices, shards(): lax.psum_scatter(stacked[2], 'dp', scatter_dimension=1, tiled=True)  173 us
    reduce_scatter x1, waiting for transfers between devices, shards(): lax.psum_scatter(stacked[0], 'dp', scatter_dimension=1, tiled=True)  155 us
    psum x1, blocking collectives, shards(): lax.psum((jnp.stack(qv_parts), jnp.stack(upb_parts)), 'dp')  81.1 us
    reduce_scatter x4, waiting for transfers between devices, reduce_branch(): lax.psum_scatter(partial_term(jnp.int32(0), local_rows * lax.axis_size('t...  40.9 us
    psum x1, blocking collectives, shards(): lax.psum((jnp.stack(gain_parts), jnp.stack(shift_parts), jnp.stack(outb_p...  39.6 us
    convert_element_type x2, other arithmetic, shards(): hidden = gelu_exact(hidden_pre).astype(jnp.bfloat16)  31.1 us
    unnamed x171, local copies, waits for them, and re-layouts  25.6 us
  transfers between devices with their start and end apart: 15, of which 13 were waited for; matrix products, arithmetic and copies ran while one was open for 11% of the time, Pallas kernels for 0%

profile of v1, /device:TPU:0, one launch (start us, length us, event | category | flops | bytes accessed | tf_op | source)
XLA Modules:
  0.0 1101.7 jit_solution(16342942065898907013)
XLA Ops:
  13.2 5.3 all_to_all.20
  37.6 11.8 %reduce-scatter.11.cloned.1.call-done = bf16[2,256,768]{2,1,0:T(8,128)(2,1)} async-done(((bf16[4,256,768]{2,1,0:T(8,128)(2,1)}), bf16[2,256,768]{2,1,0:T(8,128)(2,1)}) %reduce-scatter.11.cloned.1.call-update) | async-done | bytes 786448 | tf_op jit(solution)/shard_map/reduce_scatter | solution.py:38
  53.3 5.5 all_to_all.21
  58.8 4.1 fusion.91
  62.9 15.5 %multiply_convert_fusion.3 = (bf16[4,256,1536]{2,1,0:T(8,128)(2,1)S(1)}, f32[4,256,1536]{2,1,0:T(8,128)}) fusion(f32[4,256,1536]{2,1,0:T(8,128)S(1)} %get-tuple-element.122, f32[1536]{0:T(1024)S(1)} %get-tuple-element.73, u8[256,1536]{1,0:T(8,128)(4,1)S(1)} %get-tuple-element.51, u8[256,1536]{1,0:T(8,128)(4,1)S(1)} %get-tuple-element.50), kind=kLoop, calls=%fused_computation.40 | loop fusion | flops 111673344 | bytes 16521216 | tf_op jit(solution)/shard_map/convert_element_type | solution.py:154
  80.0 3.7 fusion.65
  83.8 10.2 reduce-scatter.13.cloned.1.call-done
  96.7 5.7 all_to_all.22
  126.5 9.8 reduce-scatter.15.cloned.1.call-done
  139.5 5.2 all_to_all.23
  144.7 4.1 fusion.92
  151.4 15.6 %multiply_convert_fusion.2 = (bf16[4,256,1536]{2,1,0:T(8,128)(2,1)}, f32[4,256,1536]{2,1,0:T(8,128)}) fusion(f32[4,256,1536]{2,1,0:T(8,128)S(1)} %get-tuple-element.125, f32[1536]{0:T(1024)S(1)} %get-tuple-element.72, u8[256,1536]{1,0:T(8,128)(4,1)S(1)} %get-tuple-element.49, u8[256,1536]{1,0:T(8,128)(4,1)S(1)} %get-tuple-element.48), kind=kLoop, calls=%fused_computation.24 | loop fusion | flops 111673344 | bytes 16521216 | tf_op jit(solution)/shard_map/convert_element_type | solution.py:154
  167.1 10.2 fusion.134
  179.0 5.4 fusion.68
  184.4 6.4 fusion.71
  191.2 3.6 reduce-scatter.19.cloned.1.call-done
  198.1 9.1 reduce-scatter.17.cloned.1.call-done
  207.2 3.4 fusion.123
  212.8 4.2 fusion.131
  217.0 3.8 copy.120
  223.9 3.4 convolution_convert_fusion.5
  229.7 8.0 multiply_reduce_fusion.1
  237.6 4.5 multiply_convert_fusion.1
  255.7 3.3 pad_maximum_fusion.3
  259.0 4.3 copy.119
  263.3 5.6 convolution_convert_fusion.3
  269.4 9.9 reduce-scatter.21.cloned.1.call-done
  284.9 11.1 %all-gather.9.cloned.1.call-done = bf16[4,256,768]{2,1,0:T(8,128)(2,1)} async-done(((bf16[2,256,768]{2,1,0:T(8,128)(2,1)}), bf16[4,256,768]{2,1,0:T(8,128)(2,1)}) %all-gather.9.cloned.1.call-update) | async-done | bytes 1572880 | tf_op jit(solution)/shard_map/all_gather | solution.py:30
  296.0 10.2 fusion.135
  308.0 5.5 fusion.62
  313.5 10.3 reduce-scatter.23.cloned.1.call-done
  333.7 8.7 all-gather.11.cloned.1.call-done
  342.3 3.6 convolution_convert_fusion.4
  348.2 5.4 multiply_reduce_fusion
  370.4 4.3 copy.130
  374.7 5.8 convolution_convert_fusion.2
  380.7 4.8 convolution_bitcast_fusion
  390.9 4.3 pad_maximum_fusion.1
  395.1 15.0 %copy.141 = f32[2,1536,768]{1,0,2:T(2,128)} copy(f32[2,1536,768]{2,1,0:T(8,128)} %pad_maximum_fusion.1) | data formatting | bytes 18874368 | tf_op jit(solution)/shard_map/stack | solution.py:257
  413.9 5.3 copy.136
  419.6 5.2 convolution_bitcast_fusion.2
  427.4 4.6 pad_maximum_fusion
  433.4 4.0 convolution_bitcast_fusion.4
  450.1 81.1 %all-reduce.3 = (f32[2,2,384]{2,1,0:T(2,128)}, f32[2,1536]{1,0:T(2,128)}) all-reduce(f32[2,2,384]{2,1,0:T(2,128)S(1)} %pad_maximum_fusion.14, f32[2,1536]{1,0:T(2,128)S(1)} %pad_maximum_fusion.13), channel_id=1, replica_groups=mesh['dp'=16,'tensor'=2] {'dp'}, use_global_device_ids=true, to_apply=%region_46.47 | all-reduce | flops 4608 | bytes 36864 | tf_op jit(solution)/shard_map/psum | solution.py:267
  535.2 39.6 %all-reduce.2 = (f32[2,2,768]{2,1,0:T(2,128)}, f32[2,2,768]{2,1,0:T(2,128)}, f32[2,2,768]{2,1,0:T(2,128)}) all-reduce(f32[2,2,768]{2,1,0:T(2,128)S(1)} %pad_maximum_fusion.10, f32[2,2,768]{2,1,0:T(2,128)S(1)} %pad_maximum_fusion.11, f32[2,2,768]{2,1,0:T(2,128)S(1)} %pad_maximum_fusion.12), channel_id=1, replica_groups=mesh['dp'=16,'tensor'=2] {'dp','tensor'}, use_global_device_ids=true, to_apply=%region_35.36 | all-reduce | flops 9216 | bytes 73728 | tf_op jit(solution)/shard_map/psum | solution.py:268
  577.6 184.9 %all-reduce.7.cloned.1.call-done = (f32[2,384,768]{1,0,2:T(2,128)}, f32[2,1536,768]{1,0,2:T(2,128)}) async-done(((f32[2,384,768]{1,0,2:T(2,128)}, f32[2,1536,768]{1,0,2:T(2,128)}), (f32[2,384,768]{1,0,2:T(2,128)}, f32[2,1536,768]{1,0,2:T(2,128)})) %all-reduce.7.cloned.1.call-update) | async-done | bytes 11796496
  766.1 173.4 %reduce-scatter.29.cloned.1.call-done = f32[2,48,1536]{2,1,0:T(8,128)} async-done(((f32[2,768,1536]{2,1,0:T(8,128)}), f32[2,48,1536]{2,1,0:T(8,128)}) %reduce-scatter.29.cloned.1.call-update) | async-done | bytes 589840 | tf_op jit(solution)/shard_map/reduce_scatter | solution.py:264
  939.5 155.1 %reduce-scatter.27.cloned.1.call-done = f32[2,48,3,384]{3,1,2,0:T(8,128)} async-done(((f32[2,768,3,384]{3,1,2,0:T(8,128)}), f32[2,48,3,384]{3,1,2,0:T(8,128)}) %reduce-scatter.27.cloned.1.call-update) | async-done | bytes 442384 | tf_op jit(solution)/shard_map/reduce_scatter | solution.py:262
  (348 shorter events, 162.1 us)
Async XLA Ops:
  7.2 42.2 %reduce-scatter.11.cloned.1.call-start = ((), (), s32[]{:S(2)}) async-start(), calls=%async_computation.14 | async-start | bytes 2359296 | tf_op jit(solution)/shard_map/reduce_scatter | solution.py:38
  13.1 5.4 copy-start.32
  23.5 5.4 copy-start.12
  25.5 4.9 copy-start.17
  25.6 4.8 copy-start.53
  35.2 14.1 %copy-start.2 = (bf16[2,256,768]{2,1,0:T(8,128)(2,1)S(1)}, bf16[2,256,768]{2,1,0:T(8,128)(2,1)}, u32[]{:S(2)}) copy-start(bf16[2,256,768]{2,1,0:T(8,128)(2,1)} %param.12) | copy-start | bytes 2359300
  37.4 56.6 %reduce-scatter.13.cloned.1.call-start = ((), (), s32[]{:S(2)}) async-start(), calls=%async_computation.15 | async-start | bytes 2359296 | tf_op jit(solution)/shard_map/reduce_scatter | solution.py:38
  49.3 9.4 slice-start.6
  52.7 6.1 slice-start.7
  53.3 26.7 %slice-start.4 = ((s8[4718592]{0:T(1024)(128)(4,1)}), s8[4194304]{0:T(1024)(128)(4,1)S(1)}, s32[]{:S(2)}) async-start(s8[4718592]{0:T(1024)(128)(4,1)} %bitcast.251), calls=%async_computation.33 | async-start | bytes 8388608
  58.8 21.2 %slice-start.5 = ((s8[4718592]{0:T(1024)(128)(4,1)}), s8[524288]{0:T(1024)(128)(4,1)S(1)}, s32[]{:S(2)}) async-start(s8[4718592]{0:T(1024)(128)(4,1)} %bitcast.251), calls=%async_computation.34 | async-start | bytes 1048576
  62.9 15.5 %copy-start.25 = (f32[4,256,1536]{2,1,0:T(8,128)}, f32[4,256,1536]{2,1,0:T(8,128)S(1)}, u32[]{:S(2)}) copy-start(f32[4,256,1536]{2,1,0:T(8,128)S(1)} %get-tuple-element.122) | copy-start | bytes 18874372
  83.6 52.7 %reduce-scatter.15.cloned.1.call-start = ((), (), s32[]{:S(2)}) async-start(), calls=%async_computation.16 | async-start | bytes 2359296 | tf_op jit(solution)/shard_map/reduce_scatter | solution.py:38
  96.6 5.8 copy-start.33
  125.9 41.1 %all-gather.5.cloned.1.call-start = ((), (), s32[]{:S(2)}) async-start(), calls=%async_computation.18 | async-start | bytes 2359296 | tf_op jit(solution)/shard_map/all_gather | solution.py:30
  126.5 68.3 %reduce-scatter.19.cloned.1.call-start = ((), (), s32[]{:S(2)}) async-start(), calls=%async_computation.19 | async-start | bytes 2359296 | tf_op jit(solution)/shard_map/reduce_scatter | solution.py:51
  136.3 8.3 slice-start.8
  139.0 5.6 slice-start.9
  184.4 22.8 %reduce-scatter.17.cloned.1.call-start = ((), (), s32[]{:S(2)}) async-start(), calls=%async_computation.17 | async-start | bytes 2359296 | tf_op jit(solution)/shard_map/reduce_scatter | solution.py:38
  190.8 33.1 %all-gather.7.cloned.1.call-start = ((), (), s32[]{:S(2)}) async-start(), calls=%async_computation.20 | async-start | bytes 2359296 | tf_op jit(solution)/shard_map/all_gather | solution.py:30
  212.7 66.6 %reduce-scatter.21.cloned.1.call-start = ((), (), s32[]{:S(2)}) async-start(), calls=%async_computation.21 | async-start | bytes 2359296 | tf_op jit(solution)/shard_map/reduce_scatter | solution.py:51
  229.7 8.0 slice-start.2
  229.7 8.0 slice-start.3
  237.6 4.5 copy-start.18
  268.9 27.1 %all-gather.9.cloned.1.call-start = ((), (), s32[]{:S(2)}) async-start(), calls=%async_computation.22 | async-start | bytes 2359296 | tf_op jit(solution)/shard_map/all_gather | solution.py:30
  284.8 39.0 %reduce-scatter.23.cloned.1.call-start = ((), (), s32[]{:S(2)}) async-start(), calls=%async_computation.23 | async-start | bytes 2359296 | tf_op jit(solution)/shard_map/reduce_scatter | solution.py:51
  308.0 15.9 %copy-start.6 = (bf16[2,256,768]{2,1,0:T(8,128)(2,1)S(1)}, bf16[2,256,768]{2,1,0:T(8,128)(2,1)}, u32[]{:S(2)}) copy-start(bf16[2,256,768]{2,1,0:T(8,128)(2,1)} %reduce-scatter.11.cloned.1.call-done) | copy-start | bytes 2359300
  313.5 28.8 %all-gather.11.cloned.1.call-start = ((), (), s32[]{:S(2)}) async-start(), calls=%async_computation.24 | async-start | bytes 2359296 | tf_op jit(solution)/shard_map/all_gather | solution.py:30
  331.1 200.0 %reduce-scatter.25.cloned.1.call-start = ((), (), s32[]{:S(2)}) async-start(), calls=%async_computation.25 | async-start | bytes 2359296 | tf_op jit(solution)/shard_map/reduce_scatter | solution.py:51
  342.3 11.3 %slice-start = ((s8[6291456]{0:T(1024)(128)(4,1)}), s8[2097152]{0:T(1024)(128)(4,1)S(1)}, s32[]{:S(2)}) async-start(s8[6291456]{0:T(1024)(128)(4,1)} %bitcast.213), calls=%async_computation.29 | async-start | bytes 4194304
  348.2 5.4 slice-start.1
  348.2 5.4 copy-start.20
  363.2 7.2 copy-start.38
  365.0 5.4 copy-start.40
  374.7 6.1 copy-start.63
  380.5 382.0 %all-reduce.7.cloned.1.call-start = ((), (), s32[]{:S(2)}) async-start(), calls=%async_computation.28 | async-start | bytes 23592960
  380.7 4.8 copy-start.64
  380.7 4.8 copy-start.71
  395.1 15.0 %copy-start.69 = (bf16[4,6,64,256]{3,2,1,0:T(8,128)(2,1)S(1)}, bf16[4,6,64,256]{3,2,1,0:T(8,128)(2,1)}, u32[]{:S(2)}) copy-start(bf16[4,6,64,256]{3,2,1,0:T(8,128)(2,1)} %copy-done.68) | copy-start | bytes 2359300
  419.3 5.5 copy-start.28
  419.3 520.3 %reduce-scatter.29.cloned.1.call-start = ((), (), s32[]{:S(2)}) async-start(), calls=%async_computation.27 | async-start | bytes 10027008 | tf_op jit(solution)/shard_map/reduce_scatter | solution.py:264
  419.6 5.2 copy-start.45
  432.0 662.6 %reduce-scatter.27.cloned.1.call-start = ((), (), s32[]{:S(2)}) async-start(), calls=%async_computation.26 | async-start | bytes 7520256 | tf_op jit(solution)/shard_map/reduce_scatter | solution.py:262
  446.0 85.2 %copy-start.50 = (f32[768]{0:T(1024)S(1)}, f32[768]{0:T(1024)}, u32[]{:S(2)}) copy-start(f32[768]{0:T(1024)} %copy-done.49) | copy-start | bytes 9220
  446.0 85.2 %copy-start.52 = (f32[2,256]{1,0:T(2,128)S(1)}, f32[2,256]{1,0:T(2,128)}, u32[]{:S(2)}) copy-start(f32[2,256]{1,0:T(2,128)} %copy-done.51) | copy-start | bytes 6148
  448.0 85.0 %copy-start.58 = (f32[2,256]{1,0:T(2,128)S(1)}, f32[2,256]{1,0:T(2,128)}, u32[]{:S(2)}) copy-start(f32[2,256]{1,0:T(2,128)} %copy-done.57) | copy-start | bytes 6148
  448.0 85.0 %copy-start.56 = (f32[2,256]{1,0:T(2,128)S(1)}, f32[2,256]{1,0:T(2,128)}, u32[]{:S(2)}) copy-start(f32[2,256]{1,0:T(2,128)} %copy-done.55) | copy-start | bytes 6148
  448.2 126.5 %copy-start.8 = (f32[2,256,768]{2,1,0:T(8,128)S(1)}, f32[2,256,768]{2,1,0:T(8,128)}, u32[]{:S(2)}) copy-start(f32[2,256,768]{2,1,0:T(8,128)} %copy-done.7) | copy-start | bytes 4718596
  (50 other events, 111.9 us)
Sparse Core Ops, SparseCore 0:
  37.6 11.7 reduce-scatter.10
  83.8 10.2 reduce-scatter.12
  126.0 10.2 reduce-scatter.14
  137.8 11.0 all-gather.4
  184.5 10.2 reduce-scatter.18
  196.9 10.2 reduce-scatter.16
  212.9 11.0 all-gather.6
  269.0 10.2 reduce-scatter.20
  285.0 10.9 all-gather.8
  313.6 10.2 reduce-scatter.22
  331.3 10.9 all-gather.10
  380.6 10.2 reduce-scatter.24
  419.4 343.0 all-reduce.6
  769.5 169.9 reduce-scatter.28
  945.3 149.2 reduce-scatter.26
